TPU v7x, 256 devices: a whole 4x4x8 slice. The times are simulated.
256 devices in a mesh: pl: 16 (over y, x), xs: 16 (over z, core).
Axes of the slice: x: 4, y: 4, z: 8, core: 2. Of those that a mesh axis runs over, the one named last changes fastest.
Arguments:
- source: float32 [512, 16, 2048], P('xs', None, 'pl'), may hold values from -6 to 6
- eastward_rate: float32 [512, 16, 2048], P('xs', None, 'pl'), may hold values from 300 to 6000
- northward_rate: float32 [512, 16, 2048], P('xs', None, 'pl'), may hold values from 300 to 6000
- vertical_rate: float32 [512, 16, 2048], P('xs', None, 'pl'), may hold values from 0.5 to 20
- amplitude: float32 [512, 16, 2048], P('xs', None, 'pl'), may hold values from 300 to 3000
Outputs:
- smoothed: float32 [512, 16, 2048], P('xs', None, 'pl')
All inputs are finite; a program needn't handle non-finite values.
Results may differ from a plain program's by a relative error of at most 0.0003.
Values sent between devices are 32-bit elements; how exact they have to be, the bound alone decides.
A program may use at most 128 MiB of HBM per device.

v0:
```python
import jax
import jax.numpy as jnp
from jax import lax
from jax.sharding import PartitionSpec as P


def cyclic(sub_band, centre, super_band, values):
    length = centre.shape[0]
    if length == 1:
        return values / centre

    def halves(operand):
        paired = operand.reshape((length // 2, 2) + operand.shape[1:])
        return (paired[:, 0], paired[:, 1])

    def following(operand, filler):
        return jnp.concatenate([operand[1:], jnp.full_like(operand[:1], filler)], axis=0)

    sub_even, sub_odd = halves(sub_band)
    centre_even, centre_odd = halves(centre)
    super_even, super_odd = halves(super_band)
    values_even, values_odd = halves(values)
    left_factor = -sub_odd / centre_even
    right_factor = -super_odd / following(centre_even, 1.0)
    reduced = cyclic(
        left_factor * sub_even,
        centre_odd + left_factor * super_even + right_factor * following(sub_even, 0.0),
        right_factor * following(super_even, 0.0),
        values_odd + left_factor * values_even + right_factor * following(values_even, 0.0),
    )
    previous = jnp.concatenate([jnp.zeros_like(reduced[:1]), reduced[:-1]], axis=0)
    even_part = (values_even - sub_even * previous - super_even * reduced) / centre_even
    return jnp.stack([even_part, reduced], axis=1).reshape((length,) + even_part.shape[1:])


def cyclic_last(sub_band, centre, super_band, values):
    length = centre.shape[-1]
    if length == 1:
        return values / centre

    def halves(operand):
        paired = operand.reshape(operand.shape[:-1] + (length // 2, 2))
        return (paired[..., 0], paired[..., 1])

    def following(operand, filler):
        return jnp.concatenate([operand[..., 1:], jnp.full_like(operand[..., :1], filler)], axis=-1)

    sub_even, sub_odd = halves(sub_band)
    centre_even, centre_odd = halves(centre)
    super_even, super_odd = halves(super_band)
    values_even, values_odd = halves(values)
    left_factor = -sub_odd / centre_even
    right_factor = -super_odd / following(centre_even, 1.0)
    reduced = cyclic_last(
        left_factor * sub_even,
        centre_odd + left_factor * super_even + right_factor * following(sub_even, 0.0),
        right_factor * following(super_even, 0.0),
        values_odd + left_factor * values_even + right_factor * following(values_even, 0.0),
    )
    previous = jnp.concatenate([jnp.zeros_like(reduced[..., :1]), reduced[..., :-1]], axis=-1)
    even_part = (values_even - sub_even * previous - super_even * reduced) / centre_even
    return jnp.stack([even_part, reduced], axis=-1).reshape(even_part.shape[:-1] + (length,))


def band_solve(values, rate_lines):
    length = values.shape[0]
    position = lax.broadcasted_iota(jnp.int32, rate_lines.shape, 0)
    sub_band = jnp.where(position > 0, -rate_lines, 0.0)
    super_band = jnp.where(position < length - 1, -rate_lines, 0.0)
    return cyclic(sub_band, 1.0 + 2.0 * rate_lines, super_band, values)


def vertical_solve(values, vertical_lines):
    return jnp.moveaxis(band_solve(jnp.moveaxis(values, 1, 0), vertical_lines), 0, 1)


def northward_solve(values, north_lines):
    length = values.shape[-1]
    position = lax.broadcasted_iota(jnp.int32, north_lines.shape, 2)
    sub_band = jnp.where(position > 0, -north_lines, 0.0)
    super_band = jnp.where(position < length - 1, -north_lines, 0.0)
    return cyclic_last(sub_band, 1.0 + 2.0 * north_lines, super_band, values)


def to_lines(values):
    return lax.all_to_all(values, "pl", split_axis=1, concat_axis=2, tiled=True)


def to_planes(values):
    return lax.all_to_all(values, "pl", split_axis=2, concat_axis=1, tiled=True)


def matrix_product(left_matrix, right_matrix):
    return (
        left_matrix[0] * right_matrix[0] + left_matrix[1] * right_matrix[2],
        left_matrix[0] * right_matrix[1] + left_matrix[1] * right_matrix[3],
        left_matrix[2] * right_matrix[0] + left_matrix[3] * right_matrix[2],
        left_matrix[2] * right_matrix[1] + left_matrix[3] * right_matrix[3],
    )


def matrix_inverse(matrix):
    determinant = matrix[0] * matrix[3] - matrix[1] * matrix[2]
    return (
        matrix[3] / determinant,
        -matrix[1] / determinant,
        -matrix[2] / determinant,
        matrix[0] / determinant,
    )


def matrix_vector(matrix, vector):
    return (
        matrix[0] * vector[0] + matrix[1] * vector[1],
        matrix[2] * vector[0] + matrix[3] * vector[1],
    )


def unpack_rows(packed):
    sub_block = (packed[0], packed[1], packed[2], packed[3])
    centre = (packed[4] + 1.0, packed[5], packed[6], packed[7] + 1.0)
    super_block = (packed[8], packed[9], packed[10], packed[11])
    right_side = (packed[12], packed[13])
    return (sub_block, centre, super_block, right_side)


def pack_rows(sub_block, centre, super_block, right_side):
    return jnp.stack(
        [
            sub_block[0],
            sub_block[1],
            sub_block[2],
            sub_block[3],
            centre[0] - 1.0,
            centre[1],
            centre[2],
            centre[3] - 1.0,
            super_block[0],
            super_block[1],
            super_block[2],
            super_block[3],
            right_side[0],
            right_side[1],
        ]
    )


def first_rows(boundary):
    blank_rows = jnp.zeros_like(boundary[0])
    return jnp.stack(
        [
            blank_rows,
            boundary[0],
            blank_rows,
            boundary[1],
            blank_rows,
            blank_rows,
            blank_rows,
            blank_rows,
            boundary[2],
            blank_rows,
            boundary[3],
            blank_rows,
            boundary[4],
            boundary[5],
        ]
    )


def eliminate(own_rows, rows_below, rows_above):
    sub_block, centre, super_block, right_side = unpack_rows(own_rows)
    sub_below, centre_below, super_below, right_below = unpack_rows(rows_below)
    sub_above, centre_above, super_above, right_above = unpack_rows(rows_above)
    left_factor = matrix_product(sub_block, matrix_inverse(centre_below))
    right_factor = matrix_product(super_block, matrix_inverse(centre_above))
    new_sub = tuple((-entry for entry in matrix_product(left_factor, sub_below)))
    new_super = tuple((-entry for entry in matrix_product(right_factor, super_above)))
    left_part = matrix_product(left_factor, super_below)
    right_part = matrix_product(right_factor, sub_above)
    new_centre = tuple((centre[slot] - left_part[slot] - right_part[slot] for slot in range(4)))
    left_vector = matrix_vector(left_factor, right_below)
    right_vector = matrix_vector(right_factor, right_above)
    new_right = (
        right_side[0] - left_vector[0] - right_vector[0],
        right_side[1] - left_vector[1] - right_vector[1],
    )
    return pack_rows(new_sub, new_centre, new_super, new_right)


def finish_rows(packed):
    sub_block, centre, super_block, right_side = unpack_rows(packed)
    return matrix_vector(matrix_inverse(centre), right_side)


def solve_gathered(gathered, own_index, devices):
    row_blocks = first_rows(jnp.moveaxis(gathered, 0, 1))
    stride = 1
    while stride < devices:
        blank_rows = jnp.zeros_like(row_blocks[:, :stride])
        rows_below = jnp.concatenate([blank_rows, row_blocks[:, :-stride]], axis=1)
        rows_above = jnp.concatenate([row_blocks[:, stride:], blank_rows], axis=1)
        row_blocks = eliminate(row_blocks, rows_below, rows_above)
        stride = stride * 2
    first_value, last_value = finish_rows(row_blocks)
    blank_value = jnp.zeros_like(first_value[:1])
    padded_first = jnp.concatenate([blank_value, first_value, blank_value], axis=0)
    padded_last = jnp.concatenate([blank_value, last_value, blank_value], axis=0)
    last_before = lax.dynamic_index_in_dim(padded_last, own_index, 0, keepdims=False)
    first_after = lax.dynamic_index_in_dim(padded_first, own_index + 2, 0, keepdims=False)
    return (last_before, first_after)


def coupled(boundary):
    devices = lax.axis_size("xs")
    gathered = lax.all_gather(boundary[None], "xs", axis=0, tiled=True)
    last_before, first_after = solve_gathered(gathered, lax.axis_index("xs"), devices)
    return (last_before, first_after)


def spike_parts(values, rate, own_index, devices):
    length = values.shape[0]
    position = lax.broadcasted_iota(jnp.int32, values.shape, 0)
    sub_band = jnp.where(position > 0, -rate, 0.0)
    super_band = jnp.where(position < length - 1, -rate, 0.0)
    centre = 1.0 + 2.0 * rate
    left_edge = jnp.where((position == 0) & (own_index > 0), -rate, 0.0)
    right_edge = jnp.where((position == length - 1) & (own_index < devices - 1), -rate, 0.0)
    stacked = jnp.stack([values, left_edge, right_edge], axis=1)
    solved = cyclic(sub_band[:, None], centre[:, None], super_band[:, None], stacked)
    particular = solved[:, 0]
    spike_left = solved[:, 1]
    spike_right = solved[:, 2]
    boundary = jnp.stack(
        [
            spike_left[0],
            spike_left[-1],
            spike_right[0],
            spike_right[-1],
            particular[0],
            particular[-1],
        ]
    )
    return (particular, spike_left, spike_right, boundary)


def eastward_solve(values, east_rate):
    particular, spike_left, spike_right, boundary = spike_parts(
        values, east_rate, lax.axis_index("xs"), lax.axis_size("xs")
    )
    last_before, first_after = coupled(boundary)
    return particular - spike_left * last_before[None] - spike_right * first_after[None]


def shards(source, eastward_rate, northward_rate, vertical_rate, amplitude):
    vertical_lines = jnp.moveaxis(vertical_rate, 1, 0)
    values = vertical_solve(source, vertical_lines)
    north_lines = lax.all_to_all(northward_rate, "pl", split_axis=1, concat_axis=2, tiled=True)
    values = to_planes(northward_solve(to_lines(values), north_lines))
    values = eastward_solve(values, eastward_rate)
    values = eastward_solve(values, eastward_rate)
    values = to_planes(northward_solve(to_lines(values), north_lines))
    values = vertical_solve(values, vertical_lines)
    return amplitude * values


def solution(mesh):
    placed = (
        P("xs", None, "pl"),
        P("xs", None, "pl"),
        P("xs", None, "pl"),
        P("xs", None, "pl"),
        P("xs", None, "pl"),
    )
    return jax.shard_map(
        shards, mesh=mesh, in_specs=placed, out_specs=P("xs", None, "pl"), check_vma=False
    )
```

profile of v0, /device:TPU:32, one launch (start us, length us, event | category | flops | bytes accessed | tf_op | source)
XLA Modules:
  0.0 218.9 jit_solution(4738351005885732317)
XLA Ops:
  0.0 1.1 fusion.12
  2.9 0.7 copy.1547
  3.7 7.0 %all-to-all-start = ((f32[32,16,128]{2,0,1:T(8,128)}), f32[32,16,128]{2,0,1:T(8,128)S(1)}, u32[]{:S(2)}, u32[]{:S(2)}) async-start(f32[32,16,128]{2,0,1:T(8,128)} %bitcast.68), calls=%async_computation | async-start | bytes 524288 | tf_op jit(solution)/shard_map/all_to_all | solution.py:86
  10.8 1.0 fusion.19
  12.7 0.9 pad_multiply_fusion.2
  13.6 0.8 copy_bitcast_fusion.6
  14.5 0.7 pad_multiply_fusion.5
  15.1 0.6 bitcast_divide_fusion.75
  15.8 0.6 pad_multiply_fusion.8
  16.4 0.6 bitcast_divide_fusion.79
  17.0 0.6 slice_bitcast_fusion.82
  17.6 0.6 slice_bitcast_fusion.83
  18.2 0.6 slice_bitcast_fusion.67
  18.8 0.6 slice_bitcast_fusion.66
  19.4 0.6 slice_bitcast_fusion.68
  20.0 0.6 slice_bitcast_fusion.42
  20.7 0.6 slice_bitcast_fusion.41
  21.3 0.6 slice_bitcast_fusion.43
  21.9 0.6 constant_dynamic-update-slice_fusion.13
  22.6 0.6 slice_bitcast_fusion.81
  23.1 0.6 multiply_bitcast_fusion.1
  23.8 0.6 slice_bitcast_fusion.97
  24.4 0.6 fusion.509
  25.0 0.6 fusion.512
  25.6 0.6 fusion.507
  26.2 0.8 copy.1550
  27.0 0.6 bitcast_divide_fusion.67
  27.6 7.4 %all-to-all-start.1 = ((f32[32,16,128]{2,0,1:T(8,128)}), f32[32,16,128]{2,0,1:T(8,128)S(1)}, u32[]{:S(2)}, u32[]{:S(2)}) async-start(f32[32,16,128]{2,0,1:T(8,128)} %copy.1550), calls=%async_computation.1 | async-start | bytes 524288 | tf_op jit(solution)/shard_map/all_to_all | solution.py:257
  35.3 1.6 fusion.580
  37.0 0.8 slice.2763
  37.8 5.9 %all-to-all-done.1 = f32[32,16,128]{2,0,1:T(8,128)S(1)} async-done(((f32[32,16,128]{2,0,1:T(8,128)}), f32[32,16,128]{2,0,1:T(8,128)S(1)}, u32[]{:S(2)}, u32[]{:S(2)}) %all-to-all-start.1) | async-done | bytes 262176 | tf_op jit(solution)/shard_map/all_to_all | solution.py:257
  44.1 1.6 fusion.579
  45.7 1.4 copy.1551
  47.2 2.6 %copy_select_fusion = (f32[32,1,1024,2]{0,2,3,1:T(8,128)S(1)}, f32[32,1,1024,2]{0,2,3,1:T(8,128)S(1)}) fusion(f32[32,1,1024,2]{0,3,2,1:T(2,128)} %bitcast.4710, pred[1024,2]{0,1:T(4,128)(4,1)S(1)} %get-tuple-element.502, pred[1024,2]{0,1:T(4,128)(4,1)S(1)} %get-tuple-element.503), kind=kLoop, calls=%fused_computation.210 | loop fusion | flops 131072 | bytes 790528 | tf_op jit(solution)/shard_map/jit(_where)/select_n | solution.py:81
  51.0 0.7 copy-done.37
  61.8 1.9 copy.1628
  63.7 0.5 broadcast.2033
  64.2 11.6 %reduce = f32[2048,32]{1,0:T(8,128)} reduce(f32[2048,1,32]{2,1,0:T(1,128)} %bitcast.4714, f32[]{:T(128)} %broadcast.2033), dimensions={1}, to_apply=%bitcast.4048.reduce_sub_computation | reduce | bytes 524292
  75.8 2.4 %reshape.3598 = f32[16,1,4096]{2,1,0:T(1,128)} reshape(f32[2048,32]{1,0:T(8,128)} %reduce) | data formatting | bytes 524288
  78.2 4.2 %all-to-all-start.2 = ((f32[16,1,4096]{2,1,0:T(1,128)}), f32[16,1,4096]{2,1,0:T(1,128)}, u32[]{:S(2)}, u32[]{:S(2)}) async-start(f32[16,1,4096]{2,1,0:T(1,128)} %reshape.3598), calls=%async_computation.2 | async-start | bytes 524288 | tf_op jit(solution)/shard_map/all_to_all | solution.py:90
  82.4 0.7 constant_dynamic-update-slice_fusion.69
  83.0 0.7 copy.2004
  83.9 1.2 copy.1632
  85.1 1.8 bitcast_divide_fusion.61
  86.9 4.2 %all-to-all-done.2 = f32[16,1,4096]{2,1,0:T(1,128)} async-done(((f32[16,1,4096]{2,1,0:T(1,128)}), f32[16,1,4096]{2,1,0:T(1,128)}, u32[]{:S(2)}, u32[]{:S(2)}) %all-to-all-start.2) | async-done | bytes 262176 | tf_op jit(solution)/shard_map/all_to_all | solution.py:90
  91.1 2.9 %reduce.1 = f32[16,4096]{1,0:T(8,128)} reduce(f32[16,1,4096]{2,1,0:T(1,128)} %all-to-all-done.2, f32[]{:T(128)} %broadcast.2033), dimensions={1}, to_apply=%all_to_all.14.reduce_sub_computation | reduce | bytes 524292 | tf_op jit(solution)/shard_map/all_to_all | solution.py:90
  93.9 3.7 %reshape.3599 = f32[2048,1,32]{2,1,0:T(1,128)} reshape(f32[16,4096]{1,0:T(8,128)} %reduce.1) | data formatting | bytes 524288
  97.7 3.4 %copy.1630 = f32[32,1,2048]{2,1,0:T(1,128)} copy(f32[32,1,2048]{0,1,2:T(1,128)} %bitcast.4711) | data formatting | bytes 524288 | tf_op jit(solution)/shard_map/all_to_all | solution.py:90
  101.1 1.0 pad_maximum_fusion.2
  104.9 20.5 %all-gather = f32[96,16,128]{2,1,0:T(8,128)S(1)} all-gather(f32[6,16,128]{2,1,0:T(8,128)S(1)} %constant_dynamic-update-slice_fusion), channel_id=2, replica_groups=mesh['pl'=16,'xs'=16] {'xs'}, dimensions={0}, use_global_device_ids=true | all-gather | bytes 835584 | tf_op jit(solution)/shard_map/all_gather | solution.py:215
  130.9 5.1 %fusion.406 = (f32[16,16,128]{2,1,0:T(8,128)S(1)}, f32[16,16,128]{2,1,0:T(8,128)S(1)}, f32[16,16,128]{2,1,0:T(8,128)S(1)}, f32[16,16,128]{2,1,0:T(8,128)S(1)}, f...) fusion(f32[16,16,128]{2,1,0:T(8,128)S(1)} %get-tuple-element.322, ...), kind=kLoop, calls=%fused_computation.1275 | loop fusion | flops 23101440 | bytes 16613376 | tf_op jit(solution)/shard_map/add | solution.py:115
  136.2 0.8 copy-done.31
  138.8 18.6 %all-gather.1 = f32[96,16,128]{2,1,0:T(8,128)S(1)} all-gather(f32[6,16,128]{2,1,0:T(8,128)S(1)} %constant_dynamic-update-slice_fusion.56), channel_id=3, replica_groups=mesh['pl'=16,'xs'=16] {'xs'}, dimensions={0}, use_global_device_ids=true | all-gather | bytes 835584 | tf_op jit(solution)/shard_map/all_gather | solution.py:215
  162.9 5.0 %fusion.403 = (f32[16,16,128]{2,1,0:T(8,128)S(1)}, f32[16,16,128]{2,1,0:T(8,128)S(1)}, f32[16,16,128]{2,1,0:T(8,128)S(1)}, f32[16,16,128]{2,1,0:T(8,128)S(1)}, f...) fusion(f32[16,16,128]{2,1,0:T(8,128)S(1)} %get-tuple-element.316, ...), kind=kLoop, calls=%fused_computation.1183 | loop fusion | flops 23101440 | bytes 16613376 | tf_op jit(solution)/shard_map/add | solution.py:115
  168.2 12.3 %all_to_all.23 = f32[32,16,128]{2,0,1:T(8,128)S(1)} all-to-all(f32[32,16,128]{2,0,1:T(8,128)S(1)} %copy.1714), channel_id=1, replica_groups=mesh['pl'=16,'xs'=16] {'pl'}, dimensions={1} | all-to-all | bytes 524288 | tf_op jit(solution)/shard_map/all_to_all | solution.py:86
  180.5 1.3 copy.1715
  181.8 2.5 %fusion.578 = (f32[32,1,1024,1]{0,3,2,1:T(1,128)S(1)}, f32[32,1,1024,1]{0,3,2,1:T(1,128)S(1)}) fusion(f32[32,1,1024,2]{0,3,2,1:T(2,128)} %bitcast.4715), kind=kLoop, calls=%fused_computation.1763 | loop fusion | bytes 524288 | tf_op jit(solution)/shard_map/slice | solution.py:43
  186.9 0.6 add_bitcast_fusion
  189.8 0.8 copy.1750
  190.6 9.3 %reduce.2 = f32[2048,32]{1,0:T(8,128)S(1)} reduce(f32[2048,1,32]{2,1,0:T(1,128)S(1)} %bitcast.4716, f32[]{:T(128)} %broadcast.2033), dimensions={1}, to_apply=%bitcast.4050.reduce_sub_computation | reduce | bytes 524292
  200.4 11.8 %all_to_all.24 = f32[16,1,4096]{2,1,0:T(1,128)S(1)} all-to-all(f32[16,1,4096]{2,1,0:T(1,128)S(1)} %reshape.3600), channel_id=1, replica_groups=mesh['pl'=16,'xs'=16] {'pl'}, dimensions={0} | all-to-all | bytes 524288 | tf_op jit(solution)/shard_map/all_to_all | solution.py:90
  212.2 1.2 reduce.3
  213.4 1.8 reshape.3601
  217.8 0.9 copy.1768
  (854 shorter events, 33.4 us)
Async XLA Ops:
  1.1 1.7 copy-start.8
  1.2 1.7 copy-start.10
  1.2 1.7 copy-start.22
  2.3 8.4 %copy-start.113 = (f32[32,16,128]{2,1,0:T(8,128)S(1)}, f32[32,16,128]{2,1,0:T(8,128)}, u32[]{:S(2)}) copy-start(f32[32,16,128]{2,1,0:T(8,128)} %param.6) | copy-start | bytes 786436
  3.7 23.9 %all-to-all-start = ((f32[32,16,128]{2,0,1:T(8,128)}), f32[32,16,128]{2,0,1:T(8,128)S(1)}, u32[]{:S(2)}, u32[]{:S(2)}) async-start(f32[32,16,128]{2,0,1:T(8,128)} %bitcast.68), calls=%async_computation | async-start | bytes 524288 | tf_op jit(solution)/shard_map/all_to_all | solution.py:86
  12.0 1.6 copy-start.59
  12.3 2.1 copy-start.39
  12.7 2.5 %copy-start.40 = (f32[16,1,1,16,128]{4,1,0,3,2:T(1,128)}, f32[16,1,1,16,128]{4,1,0,3,2:T(1,128)S(1)}, u32[]{:S(2)}) copy-start(f32[16,1,1,16,128]{4,1,0,3,2:T(1,128)S(1)} %get-tuple-element.358) | copy-start | bytes 393220
  13.6 12.6 %copy-start.112 = (f32[32,16,128]{2,1,0:T(8,128)S(1)}, f32[32,16,128]{2,1,0:T(8,128)}, u32[]{:S(2)}) copy-start(f32[32,16,128]{2,1,0:T(8,128)} %param.7) | copy-start | bytes 786436
  27.6 16.1 %all-to-all-start.1 = ((f32[32,16,128]{2,0,1:T(8,128)}), f32[32,16,128]{2,0,1:T(8,128)S(1)}, u32[]{:S(2)}, u32[]{:S(2)}) async-start(f32[32,16,128]{2,0,1:T(8,128)} %copy.1550), calls=%async_computation.1 | async-start | bytes 524288 | tf_op jit(solution)/shard_map/all_to_all | solution.py:257
  47.2 2.7 %copy-start.34 = (f32[32,1,1023]{0,2,1:T(8,128)S(1)}, f32[32,1,1023]{0,2,1:T(8,128)}, u32[]{:S(2)}) copy-start(f32[32,1,1023]{0,2,1:T(8,128)} %slice.2763) | copy-start | bytes 392836
  47.2 2.7 %copy-start.38 = (f32[32,1,1024,1]{0,3,2,1:T(1,128)S(1)}, f32[32,1,1024,1]{0,3,2,1:T(1,128)}, u32[]{:S(2)}) copy-start(f32[32,1,1024,1]{0,3,2,1:T(1,128)} %get-tuple-element.329) | copy-start | bytes 393220
  52.8 8.1 %copy-start.2 = (f32[32,1,512,1]{0,3,2,1:T(1,128)}, f32[32,1,512,1]{0,3,2,1:T(1,128)S(1)}, u32[]{:S(2)}) copy-start(f32[32,1,512,1]{0,3,2,1:T(1,128)S(1)} %get-tuple-element.347) | copy-start | bytes 196612
  53.3 7.6 %copy-start.4 = (f32[32,1,512,1]{0,3,2,1:T(1,128)}, f32[32,1,512,1]{0,3,2,1:T(1,128)S(1)}, u32[]{:S(2)}) copy-start(f32[32,1,512,1]{0,3,2,1:T(1,128)S(1)} %get-tuple-element.343) | copy-start | bytes 196612
  54.6 5.9 %copy-start.16 = (f32[32,1,256,1]{0,3,2,1:T(1,128)}, f32[32,1,256,1]{0,3,2,1:T(1,128)S(1)}, u32[]{:S(2)}) copy-start(f32[32,1,256,1]{0,3,2,1:T(1,128)S(1)} %get-tuple-element.372) | copy-start | bytes 98308
  54.8 5.7 %copy-start.18 = (f32[32,1,256,1]{0,3,2,1:T(1,128)}, f32[32,1,256,1]{0,3,2,1:T(1,128)S(1)}, u32[]{:S(2)}) copy-start(f32[32,1,256,1]{0,3,2,1:T(1,128)S(1)} %get-tuple-element.368) | copy-start | bytes 98308
  55.3 5.0 %copy-start.14 = (f32[32,1,128,1]{0,3,2,1:T(1,128)}, f32[32,1,128,1]{0,3,2,1:T(1,128)S(1)}, u32[]{:S(2)}) copy-start(f32[32,1,128,1]{0,3,2,1:T(1,128)S(1)} %get-tuple-element.399) | copy-start | bytes 49156
  55.7 4.6 %copy-start.41 = (f32[32,1,128,1]{0,3,2,1:T(1,128)}, f32[32,1,128,1]{0,3,2,1:T(1,128)S(1)}, u32[]{:S(2)}) copy-start(f32[32,1,128,1]{0,3,2,1:T(1,128)S(1)} %get-tuple-element.400) | copy-start | bytes 49156
  55.8 4.5 %copy-start.43 = (f32[32,1,128,1]{0,3,2,1:T(1,128)}, f32[32,1,128,1]{0,3,2,1:T(1,128)S(1)}, u32[]{:S(2)}) copy-start(f32[32,1,128,1]{0,3,2,1:T(1,128)S(1)} %get-tuple-element.396) | copy-start | bytes 49156
  56.1 4.0 %copy-start.35 = (f32[32,1,64,1]{0,3,2,1:T(1,128)}, f32[32,1,64,1]{0,3,2,1:T(1,128)S(1)}, u32[]{:S(2)}) copy-start(f32[32,1,64,1]{0,3,2,1:T(1,128)S(1)} %get-tuple-element.417) | copy-start | bytes 24580
  56.6 3.6 %copy-start.67 = (f32[32,1,64,1]{0,3,2,1:T(1,128)}, f32[32,1,64,1]{0,3,2,1:T(1,128)S(1)}, u32[]{:S(2)}) copy-start(f32[32,1,64,1]{0,3,2,1:T(1,128)S(1)} %get-tuple-element.418) | copy-start | bytes 24580
  56.6 3.6 %copy-start.71 = (f32[32,1,64,1]{0,3,2,1:T(1,128)}, f32[32,1,64,1]{0,3,2,1:T(1,128)S(1)}, u32[]{:S(2)}) copy-start(f32[32,1,64,1]{0,3,2,1:T(1,128)S(1)} %get-tuple-element.419) | copy-start | bytes 24580
  56.7 3.7 %copy-start.69 = (f32[32,1,64,1]{0,3,2,1:T(1,128)}, f32[32,1,64,1]{0,3,2,1:T(1,128)S(1)}, u32[]{:S(2)}) copy-start(f32[32,1,64,1]{0,3,2,1:T(1,128)S(1)} %get-tuple-element.414) | copy-start | bytes 24580
  56.7 3.7 %copy-start.100 = (f32[32,1,64]{0,2,1:T(8,128)}, f32[32,1,64]{0,2,1:T(8,128)S(1)}, u32[]{:S(2)}) copy-start(f32[32,1,64]{0,2,1:T(8,128)S(1)} %get-tuple-element.236) | copy-start | bytes 24580
  56.9 3.1 %copy-start.84 = (f32[32,1,32,1]{0,3,2,1:T(1,128)}, f32[32,1,32,1]{0,3,2,1:T(1,128)S(1)}, u32[]{:S(2)}) copy-start(f32[32,1,32,1]{0,3,2,1:T(1,128)S(1)} %get-tuple-element.433) | copy-start | bytes 12292
  56.9 3.2 %copy-start.88 = (f32[32,1,32,1]{0,3,2,1:T(1,128)}, f32[32,1,32,1]{0,3,2,1:T(1,128)S(1)}, u32[]{:S(2)}) copy-start(f32[32,1,32,1]{0,3,2,1:T(1,128)S(1)} %get-tuple-element.434) | copy-start | bytes 12292
  57.0 3.0 %copy-start.86 = (f32[32,1,32,1]{0,3,2,1:T(1,128)}, f32[32,1,32,1]{0,3,2,1:T(1,128)S(1)}, u32[]{:S(2)}) copy-start(f32[32,1,32,1]{0,3,2,1:T(1,128)S(1)} %get-tuple-element.429) | copy-start | bytes 12292
  57.1 2.9 %copy-start.82 = (f32[32,1,16,1]{0,3,2,1:T(1,128)}, f32[32,1,16,1]{0,3,2,1:T(1,128)S(1)}, u32[]{:S(2)}) copy-start(f32[32,1,16,1]{0,3,2,1:T(1,128)S(1)} %get-tuple-element.446) | copy-start | bytes 6148
  57.6 2.3 %copy-start.114 = (f32[32,1,16,1]{0,3,2,1:T(1,128)}, f32[32,1,16,1]{0,3,2,1:T(1,128)S(1)}, u32[]{:S(2)}) copy-start(f32[32,1,16,1]{0,3,2,1:T(1,128)S(1)} %get-tuple-element.447) | copy-start | bytes 6148
  57.6 2.5 %copy-start.118 = (f32[32,1,16,1]{0,3,2,1:T(1,128)}, f32[32,1,16,1]{0,3,2,1:T(1,128)S(1)}, u32[]{:S(2)}) copy-start(f32[32,1,16,1]{0,3,2,1:T(1,128)S(1)} %get-tuple-element.448) | copy-start | bytes 6148
  57.7 2.2 %copy-start.116 = (f32[32,1,16,1]{0,3,2,1:T(1,128)}, f32[32,1,16,1]{0,3,2,1:T(1,128)S(1)}, u32[]{:S(2)}) copy-start(f32[32,1,16,1]{0,3,2,1:T(1,128)S(1)} %get-tuple-element.443) | copy-start | bytes 6148
  58.3 1.8 copy-start.109
  58.4 1.8 copy-start.134
  59.3 1.6 copy-start.172
  59.3 1.6 copy-start.178
  64.2 18.8 %copy-start.60 = (f32[16,1,1,16,128]{4,1,0,3,2:T(1,128)S(1)}, f32[16,1,1,16,128]{4,1,0,3,2:T(1,128)}, u32[]{:S(2)}) copy-start(f32[16,1,1,16,128]{4,1,0,3,2:T(1,128)} %copy-done.59) | copy-start | bytes 393220
  64.2 19.5 %copy-start.64 = (f32[32,16,128]{2,0,1:T(8,128)S(1)}, f32[32,16,128]{2,0,1:T(8,128)}, u32[]{:S(2)}) copy-start(f32[32,16,128]{2,0,1:T(8,128)} %get-tuple-element.364) | copy-start | bytes 786436
  78.2 12.9 %all-to-all-start.2 = ((f32[16,1,4096]{2,1,0:T(1,128)}), f32[16,1,4096]{2,1,0:T(1,128)}, u32[]{:S(2)}, u32[]{:S(2)}) async-start(f32[16,1,4096]{2,1,0:T(1,128)} %reshape.3598), calls=%async_computation.2 | async-start | bytes 524288 | tf_op jit(solution)/shard_map/all_to_all | solution.py:90
  83.9 17.2 %copy-start.30 = (f32[32,16,128]{2,1,0:T(8,128)}, f32[32,16,128]{2,1,0:T(8,128)S(1)}, u32[]{:S(2)}) copy-start(f32[32,16,128]{2,1,0:T(8,128)S(1)} %copy.1633) | copy-start | bytes 786436
  85.1 17.0 %copy-start.32 = (f32[32,16,128]{2,1,0:T(8,128)}, f32[32,16,128]{2,1,0:T(8,128)S(1)}, u32[]{:S(2)}) copy-start(f32[32,16,128]{2,1,0:T(8,128)S(1)} %copy.1632) | copy-start | bytes 786436
  104.7 20.8 %copy-start = (f32[14,16,16,128]{3,2,1,0:T(8,128)S(1)}, f32[14,16,16,128]{3,2,1,0:T(8,128)}, u32[]{:S(2)}) copy-start(f32[14,16,16,128]{3,2,1,0:T(8,128)} %constant_dynamic-update-slice_fusion.13) | copy-start | bytes 5505028
  138.7 18.9 %copy-start.1 = (f32[14,16,16,128]{3,2,1,0:T(8,128)S(1)}, f32[14,16,16,128]{3,2,1,0:T(8,128)}, u32[]{:S(2)}) copy-start(f32[14,16,16,128]{3,2,1,0:T(8,128)} %constant_dynamic-update-slice_fusion.69) | copy-start | bytes 5505028
  181.8 2.6 %copy-start.13 = (f32[32,1,1024]{0,2,1:T(8,128)S(1)}, f32[32,1,1024]{0,2,1:T(8,128)}, u32[]{:S(2)}) copy-start(f32[32,1,1024]{0,2,1:T(8,128)} %copy-done.12) | copy-start | bytes 393220
  185.7 1.8 copy-start.173
  185.7 1.8 copy-start.175
  185.7 1.9 copy-start.167
  185.7 1.9 copy-start.169
  185.7 1.9 copy-start.155
  185.7 1.9 copy-start.157
  185.7 1.9 copy-start.161
  185.8 2.0 copy-start.135
  185.8 2.0 copy-start.137
  185.8 2.0 copy-start.115
  185.8 2.0 copy-start.117
  185.8 1.7 copy-start.177
  185.8 1.8 copy-start.179
  185.8 2.1 copy-start.85
  185.8 2.1 copy-start.87
  186.0 1.9 copy-start.68
  186.1 1.9 copy-start.70
  186.1 2.0 copy-start.42
  186.1 2.0 copy-start.44
  186.2 2.1 copy-start.17
  186.2 2.1 copy-start.19
  (121 other events, 116.1 us)
where the time goes:
time: 223 us; the launch traced here: 219 us
  other arithmetic  63.6 us (29%)
  blocking collectives  63.3 us (28%)
  local copies, waits for them, and re-layouts  57.4 us (26%)
  starting transfers between devices  18.6 us (8%)
  waiting for transfers between devices  10 us (4%)
  between operations  6 us (3%)
    all_gather x2, blocking collectives, coupled(): gathered = lax.all_gather(boundary[None], 'xs', axis=0, tiled=True)  39.2 us
    unnamed x80, other arithmetic  26.3 us
    unnamed x406, local copies, waits for them, and re-layouts  21.7 us
    all_to_all x1, blocking collectives, to_lines(): return lax.all_to_all(values, 'pl', split_axis=1, concat_axis=2, tiled=True)  12.3 us
    all_to_all x1, blocking collectives, to_planes(): return lax.all_to_all(values, 'pl', split_axis=2, concat_axis=1, tiled=True)  11.8 us
    add x2, other arithmetic, matrix_vector(): matrix[2] * vector[0] + matrix[3] * vector[1]  10.1 us
    slice x42, local copies, waits for them, and re-layouts, halves(): return (paired[..., 0], paired[..., 1])  9.86 us
    all_to_all x1, starting transfers between devices, shards(): lax.all_to_all(northward_rate, 'pl', split_axis=1, concat_axis=2, tiled=T...  7.38 us
  transfers between devices with their start and end apart: 3, of which 2 were waited for; matrix products, arithmetic and copies ran while one was open for 11% of the time, Pallas kernels for 0%

commit v1 on v0

--- a/solution.py
+++ b/solution.py
@@ -2,6 +2,11 @@
 import jax.numpy as jnp
 from jax import lax
 from jax.sharding import PartitionSpec as P
+
+
+def all_by_exchange(block, axis, along):
+    sent = jnp.stack([block] * lax.axis_size(axis))
+    return jnp.concatenate(lax.all_to_all(sent, axis, 0, 0), axis=along)
 
 
 def cyclic(sub_band, centre, super_band, values):
@@ -212,7 +217,7 @@
 
 def coupled(boundary):
     devices = lax.axis_size("xs")
-    gathered = lax.all_gather(boundary[None], "xs", axis=0, tiled=True)
+    gathered = all_by_exchange(boundary[None], "xs", 0)
     last_before, first_after = solve_gathered(gathered, lax.axis_index("xs"), devices)
     return (last_before, first_after)
 

time: 223 us -> 275 us (1.23)
  the two profiles are of different devices: /device:TPU:32 before, /device:TPU:1 now
where the time goes in v1:
time: 275 us; the launch traced here: 270 us
  local copies, waits for them, and re-layouts  83.8 us (30%)
  other arithmetic  71.3 us (26%)
  waiting for transfers between devices  51.1 us (19%)
  starting transfers between devices  35.5 us (13%)
  blocking collectives  22.2 us (8%)
  between operations  5.81 us (2%)
    all_to_all x2, waiting for transfers between devices, all_by_exchange(): return jnp.concatenate(lax.all_to_all(sent, axis, 0, 0), axis=along)  43 us
    unnamed x430, local copies, waits for them, and re-layouts  38.9 us
    unnamed x80, other arithmetic  31 us
    all_to_all x2, starting transfers between devices, all_by_exchange(): return jnp.concatenate(lax.all_to_all(sent, axis, 0, 0), axis=along)  16.9 us
    all_to_all x1, blocking collectives, to_planes(): return lax.all_to_all(values, 'pl', split_axis=2, concat_axis=1, tiled=True)  11.4 us
    add x2, other arithmetic, matrix_vector(): matrix[2] * vector[0] + matrix[3] * vector[1]  11.2 us
    all_to_all x1, blocking collectives, to_lines(): return lax.all_to_all(values, 'pl', split_axis=1, concat_axis=2, tiled=True)  10.8 us
    slice x42, local copies, waits for them, and re-layouts, halves(): return (paired[..., 0], paired[..., 1])  9.85 us
  transfers between devices with their start and end apart: 5, of which 4 were waited for; matrix products, arithmetic and copies ran while one was open for 9% of the time, Pallas kernels for 0%

profile of v1, /device:TPU:1, one launch (start us, length us, event | category | flops | bytes accessed | tf_op | source)
XLA Modules:
  0.0 269.7 jit_solution(8541832809988350474)
XLA Ops:
  0.0 1.1 fusion.12
  3.2 0.7 copy.1517
  4.0 7.6 %all-to-all-start = ((f32[32,16,128]{2,0,1:T(8,128)}), f32[32,16,128]{2,0,1:T(8,128)S(1)}, u32[]{:S(2)}, u32[]{:S(2)}) async-start(f32[32,16,128]{2,0,1:T(8,128)} %bitcast.68), calls=%async_computation | async-start | bytes 524288 | tf_op jit(solution)/shard_map/all_to_all | solution.py:91
  11.6 1.0 fusion.19
  13.6 0.9 pad_multiply_fusion.2
  14.5 0.8 copy_bitcast_fusion.6
  25.9 0.8 copy.1520
  27.3 6.8 %all-to-all-start.1 = ((f32[32,16,128]{2,0,1:T(8,128)}), f32[32,16,128]{2,0,1:T(8,128)S(1)}, u32[]{:S(2)}, u32[]{:S(2)}) async-start(f32[32,16,128]{2,0,1:T(8,128)} %copy.1520), calls=%async_computation.1 | async-start | bytes 524288 | tf_op jit(solution)/shard_map/all_to_all | solution.py:262
  34.5 1.6 fusion.580
  36.1 0.9 slice.2763
  36.9 4.7 %all-to-all-done.1 = f32[32,16,128]{2,0,1:T(8,128)S(1)} async-done(((f32[32,16,128]{2,0,1:T(8,128)}), f32[32,16,128]{2,0,1:T(8,128)S(1)}, u32[]{:S(2)}, u32[]{:S(2)}) %all-to-all-start.1) | async-done | bytes 262176 | tf_op jit(solution)/shard_map/all_to_all | solution.py:262
  42.1 1.7 fusion.579
  43.7 1.3 copy.1521
  45.1 2.6 copy_select_fusion
  48.9 0.7 copy-done.35
  59.7 1.8 copy.1598
  62.0 11.6 %reduce = f32[2048,32]{1,0:T(8,128)} reduce(f32[2048,1,32]{2,1,0:T(1,128)} %bitcast.4702, f32[]{:T(128)} %broadcast.2037), dimensions={1}, to_apply=%bitcast.4049.reduce_sub_computation | reduce | bytes 524292
  73.6 2.4 reshape.3608
  76.0 4.2 %all-to-all-start.2 = ((f32[16,1,4096]{2,1,0:T(1,128)}), f32[16,1,4096]{2,1,0:T(1,128)}, u32[]{:S(2)}, u32[]{:S(2)}) async-start(f32[16,1,4096]{2,1,0:T(1,128)} %reshape.3608), calls=%async_computation.2 | async-start | bytes 524288 | tf_op jit(solution)/shard_map/all_to_all | solution.py:95
  80.9 0.7 copy.1974
  81.7 1.1 copy.1602
  82.8 1.7 bitcast_divide_fusion.61
  84.5 3.4 %all-to-all-done.2 = f32[16,1,4096]{2,1,0:T(1,128)} async-done(((f32[16,1,4096]{2,1,0:T(1,128)}), f32[16,1,4096]{2,1,0:T(1,128)}, u32[]{:S(2)}, u32[]{:S(2)}) %all-to-all-start.2) | async-done | bytes 262176 | tf_op jit(solution)/shard_map/all_to_all | solution.py:95
  87.9 2.9 %reduce.1 = f32[16,4096]{1,0:T(8,128)} reduce(f32[16,1,4096]{2,1,0:T(1,128)} %all-to-all-done.2, f32[]{:T(128)} %broadcast.2037), dimensions={1}, to_apply=%all_to_all.18.reduce_sub_computation | reduce | bytes 524292 | tf_op jit(solution)/shard_map/all_to_all | solution.py:95
  90.8 3.8 %reshape.3609 = f32[2048,1,32]{2,1,0:T(1,128)} reshape(f32[16,4096]{1,0:T(8,128)} %reduce.1) | data formatting | bytes 524288
  94.5 3.4 %copy.1600 = f32[32,1,2048]{2,1,0:T(1,128)} copy(f32[32,1,2048]{0,1,2:T(1,128)} %bitcast.4699) | data formatting | bytes 524288 | tf_op jit(solution)/shard_map/all_to_all | solution.py:95
  98.0 1.0 pad_maximum_fusion.2
  101.8 0.9 copy-done.14
  102.7 1.0 stack.418
  103.7 12.7 %all-to-all-start.3 = ((f32[16,1,6,16,128]{4,3,2,1,0:T(8,128)}), f32[16,1,6,16,128]{4,3,2,1,0:T(8,128)}, u32[]{:S(2)}, u32[]{:S(2)}) async-start(f32[16,1,6,16,128]{4,3,2,1,0:T(8,128)} %stack.418), calls=%async_computation.3 | async-start | bytes 1572864 | tf_op jit(solution)/shard_map/all_to_all | solution.py:9
  117.1 21.9 %all-to-all-done.3 = f32[16,1,6,16,128]{4,3,2,1,0:T(8,128)} async-done(((f32[16,1,6,16,128]{4,3,2,1,0:T(8,128)}), f32[16,1,6,16,128]{4,3,2,1,0:T(8,128)}, u32[]{:S(2)}, u32[]{:S(2)}) %all-to-all-start.3) | async-done | bytes 786464 | tf_op jit(solution)/shard_map/all_to_all | solution.py:9
  139.0 1.6 constant_dynamic-update-slice_fusion.12
  141.3 1.6 constant_dynamic-update-slice_fusion.10
  142.8 0.8 broadcast_dynamic-update-slice_fusion.1
  143.7 1.6 constant_dynamic-update-slice_fusion.9
  145.9 1.6 constant_dynamic-update-slice_fusion.7
  148.1 1.7 copy_dynamic-update-slice_fusion
  149.7 2.3 fusion.576
  152.1 1.0 constant_dynamic-update-slice_fusion.27
  153.1 1.0 constant_dynamic-update-slice_fusion.25
  154.2 1.4 fusion.103
  155.6 1.0 constant_dynamic-update-slice_fusion.23
  156.7 1.0 constant_dynamic-update-slice_fusion.21
  158.0 1.0 constant_dynamic-update-slice_fusion.15
  159.0 1.0 constant_dynamic-update-slice_fusion.14
  163.5 6.2 %fusion.406 = (f32[16,16,128]{2,1,0:T(8,128)S(1)}, f32[16,16,128]{2,1,0:T(8,128)S(1)}, f32[16,16,128]{2,1,0:T(8,128)S(1)}, f32[16,16,128]{2,1,0:T(8,128)S(1)}, f...) fusion(f32[16,16,128]{2,1,0:T(8,128)S(1)} %get-tuple-element.322, ...), kind=kLoop, calls=%fused_computation.1275 | loop fusion | flops 23101440 | bytes 16613376 | tf_op jit(solution)/shard_map/add | solution.py:120
  173.3 0.9 copy-done.16
  174.2 1.0 stack.435
  175.2 4.2 %all-to-all-start.4 = ((f32[16,1,6,16,128]{4,3,2,1,0:T(8,128)}), f32[16,1,6,16,128]{4,3,2,1,0:T(8,128)}, u32[]{:S(2)}, u32[]{:S(2)}) async-start(f32[16,1,6,16,128]{4,3,2,1,0:T(8,128)} %stack.435), calls=%async_computation.4 | async-start | bytes 1572864 | tf_op jit(solution)/shard_map/all_to_all | solution.py:9
  180.0 21.1 %all-to-all-done.4 = f32[16,1,6,16,128]{4,3,2,1,0:T(8,128)} async-done(((f32[16,1,6,16,128]{4,3,2,1,0:T(8,128)}), f32[16,1,6,16,128]{4,3,2,1,0:T(8,128)}, u32[]{:S(2)}, u32[]{:S(2)}) %all-to-all-start.4) | async-done | bytes 786464 | tf_op jit(solution)/shard_map/all_to_all | solution.py:9
  201.1 1.2 copy.1973
  204.3 0.8 broadcast_dynamic-update-slice_fusion
  207.8 0.7 slice_dynamic-update-slice_fusion
  208.5 2.3 fusion.572
  215.6 5.0 %fusion.403 = (f32[16,16,128]{2,1,0:T(8,128)S(1)}, f32[16,16,128]{2,1,0:T(8,128)S(1)}, f32[16,16,128]{2,1,0:T(8,128)S(1)}, f32[16,16,128]{2,1,0:T(8,128)S(1)}, f...) fusion(f32[16,16,128]{2,1,0:T(8,128)S(1)} %get-tuple-element.316, ...), kind=kLoop, calls=%fused_computation.1183 | loop fusion | flops 23101440 | bytes 16613376 | tf_op jit(solution)/shard_map/add | solution.py:120
  220.9 10.8 %all_to_all.58 = f32[32,16,128]{2,0,1:T(8,128)S(1)} all-to-all(f32[32,16,128]{2,0,1:T(8,128)S(1)} %copy.1684), channel_id=1, replica_groups=mesh['pl'=16,'xs'=16] {'pl'}, dimensions={1} | all-to-all | bytes 524288 | tf_op jit(solution)/shard_map/all_to_all | solution.py:91
  231.7 1.3 copy.1685
  233.1 2.5 fusion.578
  241.0 0.8 copy.1720
  241.8 9.3 %reduce.2 = f32[2048,32]{1,0:T(8,128)S(1)} reduce(f32[2048,1,32]{2,1,0:T(1,128)S(1)} %bitcast.4704, f32[]{:T(128)} %broadcast.2037), dimensions={1}, to_apply=%bitcast.4051.reduce_sub_computation | reduce | bytes 524292
  251.6 11.4 %all_to_all.59 = f32[16,1,4096]{2,1,0:T(1,128)S(1)} all-to-all(f32[16,1,4096]{2,1,0:T(1,128)S(1)} %reshape.3610), channel_id=1, replica_groups=mesh['pl'=16,'xs'=16] {'pl'}, dimensions={0} | all-to-all | bytes 524288 | tf_op jit(solution)/shard_map/all_to_all | solution.py:95
  263.0 1.2 reduce.3
  264.3 1.8 reshape.3611
  268.6 0.9 copy.1738
  (882 shorter events, 54.2 us)
Async XLA Ops:
  1.1 1.9 copy-start.6
  1.2 1.9 copy-start.8
  1.2 1.9 copy-start.24
  2.9 8.6 %copy-start.121 = (f32[32,16,128]{2,1,0:T(8,128)S(1)}, f32[32,16,128]{2,1,0:T(8,128)}, u32[]{:S(2)}) copy-start(f32[32,16,128]{2,1,0:T(8,128)} %param.6) | copy-start | bytes 786436
  4.0 23.3 %all-to-all-start = ((f32[32,16,128]{2,0,1:T(8,128)}), f32[32,16,128]{2,0,1:T(8,128)S(1)}, u32[]{:S(2)}, u32[]{:S(2)}) async-start(f32[32,16,128]{2,0,1:T(8,128)} %bitcast.68), calls=%async_computation | async-start | bytes 524288 | tf_op jit(solution)/shard_map/all_to_all | solution.py:91
  13.2 2.1 copy-start.37
  13.5 2.5 copy-start.38
  14.4 11.4 %copy-start.120 = (f32[32,16,128]{2,1,0:T(8,128)S(1)}, f32[32,16,128]{2,1,0:T(8,128)}, u32[]{:S(2)}) copy-start(f32[32,16,128]{2,1,0:T(8,128)} %param.7) | copy-start | bytes 786436
  17.9 9.4 %copy-start.164 = (f32[1,2,1,16,128]{4,3,2,1,0:T(8,128)}, f32[1,2,1,16,128]{4,3,2,1,0:T(8,128)S(1)}, u32[]{:S(2)}) copy-start(f32[1,2,1,16,128]{4,3,2,1,0:T(8,128)S(1)} %fusion.497) | copy-start | bytes 49156
  27.3 14.4 %all-to-all-start.1 = ((f32[32,16,128]{2,0,1:T(8,128)}), f32[32,16,128]{2,0,1:T(8,128)S(1)}, u32[]{:S(2)}, u32[]{:S(2)}) async-start(f32[32,16,128]{2,0,1:T(8,128)} %copy.1520), calls=%async_computation.1 | async-start | bytes 524288 | tf_op jit(solution)/shard_map/all_to_all | solution.py:262
  45.1 2.7 copy-start.32
  45.1 2.7 copy-start.36
  50.7 8.1 %copy-start = (f32[32,1,512,1]{0,3,2,1:T(1,128)}, f32[32,1,512,1]{0,3,2,1:T(1,128)S(1)}, u32[]{:S(2)}) copy-start(f32[32,1,512,1]{0,3,2,1:T(1,128)S(1)} %get-tuple-element.347) | copy-start | bytes 196612
  51.2 7.6 %copy-start.2 = (f32[32,1,512,1]{0,3,2,1:T(1,128)}, f32[32,1,512,1]{0,3,2,1:T(1,128)S(1)}, u32[]{:S(2)}) copy-start(f32[32,1,512,1]{0,3,2,1:T(1,128)S(1)} %get-tuple-element.343) | copy-start | bytes 196612
  52.5 5.9 %copy-start.18 = (f32[32,1,256,1]{0,3,2,1:T(1,128)}, f32[32,1,256,1]{0,3,2,1:T(1,128)S(1)}, u32[]{:S(2)}) copy-start(f32[32,1,256,1]{0,3,2,1:T(1,128)S(1)} %get-tuple-element.372) | copy-start | bytes 98308
  52.8 5.7 %copy-start.20 = (f32[32,1,256,1]{0,3,2,1:T(1,128)}, f32[32,1,256,1]{0,3,2,1:T(1,128)S(1)}, u32[]{:S(2)}) copy-start(f32[32,1,256,1]{0,3,2,1:T(1,128)S(1)} %get-tuple-element.368) | copy-start | bytes 98308
  53.2 5.0 %copy-start.12 = (f32[32,1,128,1]{0,3,2,1:T(1,128)}, f32[32,1,128,1]{0,3,2,1:T(1,128)S(1)}, u32[]{:S(2)}) copy-start(f32[32,1,128,1]{0,3,2,1:T(1,128)S(1)} %get-tuple-element.399) | copy-start | bytes 49156
  53.6 4.6 %copy-start.39 = (f32[32,1,128,1]{0,3,2,1:T(1,128)}, f32[32,1,128,1]{0,3,2,1:T(1,128)S(1)}, u32[]{:S(2)}) copy-start(f32[32,1,128,1]{0,3,2,1:T(1,128)S(1)} %get-tuple-element.400) | copy-start | bytes 49156
  53.8 4.5 %copy-start.41 = (f32[32,1,128,1]{0,3,2,1:T(1,128)}, f32[32,1,128,1]{0,3,2,1:T(1,128)S(1)}, u32[]{:S(2)}) copy-start(f32[32,1,128,1]{0,3,2,1:T(1,128)S(1)} %get-tuple-element.396) | copy-start | bytes 49156
  54.0 4.0 %copy-start.33 = (f32[32,1,64,1]{0,3,2,1:T(1,128)}, f32[32,1,64,1]{0,3,2,1:T(1,128)S(1)}, u32[]{:S(2)}) copy-start(f32[32,1,64,1]{0,3,2,1:T(1,128)S(1)} %get-tuple-element.417) | copy-start | bytes 24580
  54.5 3.7 %copy-start.70 = (f32[32,1,64,1]{0,3,2,1:T(1,128)}, f32[32,1,64,1]{0,3,2,1:T(1,128)S(1)}, u32[]{:S(2)}) copy-start(f32[32,1,64,1]{0,3,2,1:T(1,128)S(1)} %get-tuple-element.418) | copy-start | bytes 24580
  54.5 3.7 %copy-start.74 = (f32[32,1,64,1]{0,3,2,1:T(1,128)}, f32[32,1,64,1]{0,3,2,1:T(1,128)S(1)}, u32[]{:S(2)}) copy-start(f32[32,1,64,1]{0,3,2,1:T(1,128)S(1)} %get-tuple-element.419) | copy-start | bytes 24580
  54.6 3.7 %copy-start.72 = (f32[32,1,64,1]{0,3,2,1:T(1,128)}, f32[32,1,64,1]{0,3,2,1:T(1,128)S(1)}, u32[]{:S(2)}) copy-start(f32[32,1,64,1]{0,3,2,1:T(1,128)S(1)} %get-tuple-element.414) | copy-start | bytes 24580
  54.6 3.7 %copy-start.108 = (f32[32,1,64]{0,2,1:T(8,128)}, f32[32,1,64]{0,2,1:T(8,128)S(1)}, u32[]{:S(2)}) copy-start(f32[32,1,64]{0,2,1:T(8,128)S(1)} %get-tuple-element.236) | copy-start | bytes 24580
  54.8 3.1 %copy-start.92 = (f32[32,1,32,1]{0,3,2,1:T(1,128)}, f32[32,1,32,1]{0,3,2,1:T(1,128)S(1)}, u32[]{:S(2)}) copy-start(f32[32,1,32,1]{0,3,2,1:T(1,128)S(1)} %get-tuple-element.433) | copy-start | bytes 12292
  54.8 3.2 %copy-start.96 = (f32[32,1,32,1]{0,3,2,1:T(1,128)}, f32[32,1,32,1]{0,3,2,1:T(1,128)S(1)}, u32[]{:S(2)}) copy-start(f32[32,1,32,1]{0,3,2,1:T(1,128)S(1)} %get-tuple-element.434) | copy-start | bytes 12292
  54.9 3.0 %copy-start.94 = (f32[32,1,32,1]{0,3,2,1:T(1,128)}, f32[32,1,32,1]{0,3,2,1:T(1,128)S(1)}, u32[]{:S(2)}) copy-start(f32[32,1,32,1]{0,3,2,1:T(1,128)S(1)} %get-tuple-element.429) | copy-start | bytes 12292
  55.1 2.9 %copy-start.90 = (f32[32,1,16,1]{0,3,2,1:T(1,128)}, f32[32,1,16,1]{0,3,2,1:T(1,128)S(1)}, u32[]{:S(2)}) copy-start(f32[32,1,16,1]{0,3,2,1:T(1,128)S(1)} %get-tuple-element.446) | copy-start | bytes 6148
  55.5 2.3 copy-start.122
  55.6 2.5 copy-start.126
  55.6 2.3 copy-start.124
  56.2 1.9 copy-start.117
  56.3 1.8 copy-start.142
  62.0 18.2 %copy-start.165 = (f32[1,2,1,16,128]{4,3,2,1,0:T(8,128)S(1)}, f32[1,2,1,16,128]{4,3,2,1,0:T(8,128)}, u32[]{:S(2)}) copy-start(f32[1,2,1,16,128]{4,3,2,1,0:T(8,128)} %copy-done.164) | copy-start | bytes 49156
  62.0 18.8 %copy-start.60 = (f32[16,1,1,16,128]{4,1,0,3,2:T(1,128)S(1)}, f32[16,1,1,16,128]{4,1,0,3,2:T(1,128)}, u32[]{:S(2)}) copy-start(f32[16,1,1,16,128]{4,1,0,3,2:T(1,128)} %copy-done.59) | copy-start | bytes 393220
  62.0 19.5 %copy-start.67 = (f32[32,16,128]{2,0,1:T(8,128)S(1)}, f32[32,16,128]{2,0,1:T(8,128)}, u32[]{:S(2)}) copy-start(f32[32,16,128]{2,0,1:T(8,128)} %get-tuple-element.364) | copy-start | bytes 786436
  76.0 11.8 %all-to-all-start.2 = ((f32[16,1,4096]{2,1,0:T(1,128)}), f32[16,1,4096]{2,1,0:T(1,128)}, u32[]{:S(2)}, u32[]{:S(2)}) async-start(f32[16,1,4096]{2,1,0:T(1,128)} %reshape.3608), calls=%async_computation.2 | async-start | bytes 524288 | tf_op jit(solution)/shard_map/all_to_all | solution.py:95
  103.7 35.4 %all-to-all-start.3 = ((f32[16,1,6,16,128]{4,3,2,1,0:T(8,128)}), f32[16,1,6,16,128]{4,3,2,1,0:T(8,128)}, u32[]{:S(2)}, u32[]{:S(2)}) async-start(f32[16,1,6,16,128]{4,3,2,1,0:T(8,128)} %stack.418), calls=%async_computation.3 | async-start | bytes 1572864 | tf_op jit(solution)/shard_map/all_to_all | solution.py:9
  163.5 6.3 %copy-start.15 = (f32[16,2,3,16,128]{4,3,2,1,0:T(8,128)S(1)}, f32[16,2,3,16,128]{4,3,2,1,0:T(8,128)}, u32[]{:S(2)}) copy-start(f32[16,2,3,16,128]{4,3,2,1,0:T(8,128)} %copy-done.14) | copy-start | bytes 2359300
  175.2 25.9 %all-to-all-start.4 = ((f32[16,1,6,16,128]{4,3,2,1,0:T(8,128)}), f32[16,1,6,16,128]{4,3,2,1,0:T(8,128)}, u32[]{:S(2)}, u32[]{:S(2)}) async-start(f32[16,1,6,16,128]{4,3,2,1,0:T(8,128)} %stack.435), calls=%async_computation.4 | async-start | bytes 1572864 | tf_op jit(solution)/shard_map/all_to_all | solution.py:9
  215.6 5.1 %copy-start.159 = (f32[1,16,128]{2,1,0:T(8,128)S(1)}, f32[1,16,128]{2,1,0:T(8,128)}, u32[]{:S(2)}) copy-start(f32[1,16,128]{2,1,0:T(8,128)} %copy-done.158) | copy-start | bytes 24580
  215.6 5.2 %copy-start.17 = (f32[16,2,3,16,128]{4,3,2,1,0:T(8,128)S(1)}, f32[16,2,3,16,128]{4,3,2,1,0:T(8,128)}, u32[]{:S(2)}) copy-start(f32[16,2,3,16,128]{4,3,2,1,0:T(8,128)} %copy-done.16) | copy-start | bytes 2359300
  233.1 2.6 copy-start.11
  236.9 1.8 copy-start.185
  236.9 1.8 copy-start.187
  236.9 1.9 copy-start.179
  236.9 1.9 copy-start.181
  236.9 1.9 copy-start.167
  236.9 1.9 copy-start.169
  237.0 1.9 copy-start.173
  237.0 2.0 copy-start.143
  237.0 2.0 copy-start.145
  237.0 2.0 copy-start.123
  237.0 2.0 copy-start.125
  237.0 1.7 copy-start.189
  237.0 1.8 copy-start.191
  237.0 2.1 copy-start.93
  237.0 2.1 copy-start.95
  237.3 1.9 copy-start.71
  237.3 1.9 copy-start.73
  237.3 2.0 copy-start.40
  237.3 2.0 copy-start.42
  237.4 2.1 copy-start.19
  237.4 2.1 copy-start.21
  (135 other events, 136.7 us)
